TPU v7x, 32 devices: a whole 2x2x4 slice. The times are simulated.
32 devices in a mesh: col: 16 (over z, x, core), orb: 2 (over y).
Axes of the slice: x: 2, y: 2, z: 4, core: 2. Of those that a mesh axis runs over, the one named last changes fastest.
Arguments:
- slab_occ: bfloat16 [1024, 400], P('col', 'orb'), may hold values from -6 to 6
- slab_vir: bfloat16 [1024, 2400], P('col', 'orb'), may hold values from -6 to 6
- orbitals_occ: bfloat16 [400, 16384], P('orb', 'col'), may hold values from -0.3125 to 0.3125
- orbitals_vir: bfloat16 [2400, 16384], P('orb', 'col'), may hold values from -0.125 to 0.125
- occ_energy: float32 [400], P('orb'), may hold values from -2 to -0.1
- vir_energy: float32 [2400], P('orb'), may hold values from 0.1 to 3
- screened: bfloat16 [1024, 16384], P('col'), may hold values from -6 to 6
Outputs:
- occ_kernel: bfloat16 [1024, 400], P(('col', 'orb'))
- vir_kernel: bfloat16 [1024, 2400], P(('col', 'orb'))
All inputs are finite; a program needn't handle non-finite values.
Results may differ from a plain program's by a relative error of at most 0.014.
Values may be sent and summed in bfloat16 or wider, within the bound.
A program may use at most 64 MiB of HBM per device.

v0:
```python
import jax
import jax.numpy as jnp
from jax import lax
from jax.sharding import PartitionSpec as P


def local(slab_occ, slab_vir, orbitals_occ, orbitals_vir, occ_energy, vir_energy, screened):
    n_orb = lax.axis_size("orb")
    n_col = lax.axis_size("col")
    part = lax.axis_index("orb")
    block = slab_occ.shape[0] // n_orb
    columns = orbitals_occ.shape[1]
    all_occ, all_vir, energy_occ, energy_vir = (
        lax.all_gather(orbitals_occ, "orb", axis=0, tiled=True),
        lax.all_gather(orbitals_vir, "orb", axis=0, tiled=True),
        lax.all_gather(occ_energy.astype(jnp.bfloat16), "orb", axis=0, tiled=True).astype(
            occ_energy.dtype
        ),
        lax.all_gather(vir_energy.astype(jnp.bfloat16), "orb", axis=0, tiled=True).astype(
            vir_energy.dtype
        ),
    )
    near_occ, near_vir = (
        lax.all_gather(slab_occ, "col", axis=0, tiled=True),
        lax.all_gather(slab_vir, "col", axis=0, tiled=True),
    )
    scaled_occ = (near_occ.astype(jnp.float32) * jnp.exp(occ_energy)[None, :]).astype(jnp.bfloat16)
    scaled_vir = (near_vir.astype(jnp.float32) * jnp.exp(-vir_energy)[None, :]).astype(jnp.bfloat16)
    part_occ = jnp.dot(scaled_occ, orbitals_occ, preferred_element_type=jnp.float32)
    part_vir = jnp.dot(scaled_vir, orbitals_vir, preferred_element_type=jnp.float32)
    shape_three = (n_col, n_orb, block * columns)
    green_occ, green_vir = (
        lax.psum_scatter(
            part_occ.reshape(shape_three).astype(jnp.bfloat16),
            "orb",
            scatter_dimension=1,
            tiled=True,
        ).astype(jnp.float32),
        lax.psum_scatter(
            part_vir.reshape(shape_three).astype(jnp.bfloat16),
            "orb",
            scatter_dimension=1,
            tiled=True,
        ).astype(jnp.float32),
    )
    green_occ = green_occ.reshape((n_col * block, columns))
    green_vir = green_vir.reshape((n_col * block, columns))
    arrived = lax.all_to_all(screened, "col", split_axis=1, concat_axis=0, tiled=True)
    shaped = arrived.reshape((n_col, n_orb, block, arrived.shape[1]))
    picked = lax.dynamic_index_in_dim(shaped, part, 1, keepdims=False)
    screen = picked.reshape((n_col * block, arrived.shape[1]))
    screen_float = screen.astype(jnp.float32)
    occ_side = (green_vir * screen_float).astype(jnp.bfloat16)
    vir_side = (green_occ * screen_float).astype(jnp.bfloat16)
    dims = (((1,), (1,)), ((), ()))
    occ_term = lax.dot_general(occ_side, all_occ, dims, preferred_element_type=jnp.float32)
    vir_term = lax.dot_general(vir_side, all_vir, dims, preferred_element_type=jnp.float32)
    terms = lax.psum_scatter(
        jnp.concatenate([occ_term, vir_term], axis=1), "col", scatter_dimension=0, tiled=True
    )
    n_occ = all_occ.shape[0]
    return (terms[:, :n_occ].astype(jnp.bfloat16), terms[:, n_occ:].astype(jnp.bfloat16))


def solution(mesh):
    return jax.shard_map(
        local,
        mesh=mesh,
        in_specs=(
            P("col", "orb"),
            P("col", "orb"),
            P("orb", "col"),
            P("orb", "col"),
            P("orb"),
            P("orb"),
            P("col", None),
        ),
        out_specs=(P(("col", "orb"), None), P(("col", "orb"), None)),
        check_vma=False,
    )
```

profile of v0, /device:TPU:0, one launch (start us, length us, event | category | flops | bytes accessed | tf_op | source)
XLA Modules:
  0.0 265.2 jit_solution(14562446115532822757)
XLA Ops:
  8.0 0.7 all-gather.3.cloned.1.call-update
  8.8 0.7 exp.7
  9.5 25.2 %all_gather.14 = bf16[1024,200]{1,0:T(8,128)(2,1)S(1)} all-gather(bf16[64,200]{1,0:T(8,128)(2,1)} %param.7), channel_id=1, replica_groups=mesh['col'=16,'orb'=2] {'col'}, dimensions={0}, use_global_device_ids=true | all-gather | bytes 435200 | tf_op jit(solution)/shard_map/all_gather | solution.py:24
  34.6 1.7 convolution_convert_fusion
  36.4 2.8 %convert_element_type.50 = bf16[16,2,32768]{2,1,0:T(2,128)(2,1)} reshape(bf16[1024,1024]{1,0:T(8,128)(2,1)S(1)} %convolution_convert_fusion) | data formatting | bytes 4194304 | tf_op jit(solution)/shard_map/convert_element_type | solution.py:34
  39.1 4.3 %copy.18 = bf16[16,2,32768]{2,0,1:T(8,128)(2,1)} copy(bf16[16,2,32768]{2,1,0:T(2,128)(2,1)} %convert_element_type.50) | data formatting | bytes 4194304 | tf_op jit(solution)/shard_map/convert_element_type | solution.py:34
  43.5 0.7 all-gather.5.cloned.1.call-update
  44.2 0.8 copy-done.1
  45.0 1.6 copy.25
  46.6 4.7 %all-to-all-start = ((bf16[64,16,1024]{2,0,1:T(8,128)(2,1)}), bf16[64,16,1024]{2,0,1:T(8,128)(2,1)}, u32[]{:S(2)}, u32[]{:S(2)}) async-start(bf16[64,16,1024]{2,0,1:T(8,128)(2,1)} %bitcast.17), calls=%async_computation.1 | async-start | bytes 4194304 | tf_op jit(solution)/shard_map/all_to_all | solution.py:48
  51.3 0.0 reduce-scatter.6.cloned.1.call-start
  51.4 12.7 %all-gather.3.cloned.1.call-done = bf16[1024,1200]{1,0:T(8,128)(2,1)} async-done(((bf16[64,1200]{1,0:T(8,128)(2,1)}), bf16[1024,1200]{1,0:T(8,128)(2,1)}) %all-gather.3.cloned.1.call-update) | async-done | bytes 2457616 | tf_op jit(solution)/shard_map/all_gather | solution.py:25
  64.1 5.9 %fusion.4 = bf16[1024,1024]{1,0:T(8,128)(2,1)} fusion(bf16[1200,1024]{1,0:T(8,128)(2,1)S(1)} %copy-done, bf16[1024,1200]{1,0:T(8,128)(2,1)} %all-gather.3.cloned.1.call-done, f32[1200]{0:T(1024)S(1)} %negate_exponential_fusion), kind=kOutput, calls=%fused_computation.9 | convolution fusion | flops 2521317376 | bytes 7017152 | tf_op jit(solution)/shard_map/dot_general | solution.py:30
  70.0 3.5 %convert_element_type.43 = bf16[16,2,32768]{2,1,0:T(2,128)(2,1)S(1)} reshape(bf16[1024,1024]{1,0:T(8,128)(2,1)} %fusion.4) | data formatting | bytes 4194304 | tf_op jit(solution)/shard_map/convert_element_type | solution.py:40
  73.5 2.5 copy.16
  76.1 21.7 %all_gather.13 = bf16[400,1024]{1,0:T(8,128)(2,1)} all-gather(bf16[200,1024]{1,0:T(8,128)(2,1)S(1)} %copy-done.2), channel_id=1, replica_groups=mesh['col'=16,'orb'=2] {'orb'}, dimensions={0}, use_global_device_ids=true | all-gather | bytes 1228800 | tf_op jit(solution)/shard_map/all_gather | solution.py:14
  97.8 1.3 constant_dynamic-slice_fusion
  99.2 1.5 reshape.42
  100.7 36.1 %all-gather.5.cloned.1.call-done = bf16[2400,1024]{1,0:T(8,128)(2,1)} async-done(((bf16[1200,1024]{1,0:T(8,128)(2,1)}), bf16[2400,1024]{1,0:T(8,128)(2,1)}) %all-gather.5.cloned.1.call-update) | async-done | bytes 4915216 | tf_op jit(solution)/shard_map/all_gather | solution.py:15
  136.8 6.9 %fusion.5 = f32[512,2400]{0,1:T(8,128)} fusion(bf16[2400,1024]{1,0:T(8,128)(2,1)} %all-gather.5.cloned.1.call-done, f32[512,1024]{1,0:T(8,128)S(1)} %reshape.42, bf16[512,1024]{1,0:T(8,128)(2,1)S(1)} %bitcast.18), kind=kOutput, calls=%fused_computation.11 | convolution fusion | flops 2518155264 | bytes 12976128 | tf_op jit(solution)/shard_map/dot_general | solution.py:57
  143.6 16.5 %reduce-scatter.6.cloned.1.call-done = bf16[16,1,32768]{2,0,1:T(8,128)(2,1)} async-done(((bf16[16,2,32768]{2,0,1:T(8,128)(2,1)}), bf16[16,1,32768]{2,0,1:T(8,128)(2,1)}) %reduce-scatter.6.cloned.1.call-update) | async-done | bytes 1048592 | tf_op jit(solution)/shard_map/reduce_scatter | solution.py:39
  160.1 1.5 reshape.39
  161.6 1.8 fusion.7
  163.4 5.6 %pad_maximum_fusion = f32[512,2800]{0,1:T(8,128)} fusion(f32[512,2400]{0,1:T(8,128)} %fusion.5, f32[512,400]{0,1:T(8,128)S(1)} %fusion.7), kind=kLoop, calls=%fused_computation | loop fusion | flops 1433600 | bytes 11468800 | tf_op jit(solution)/shard_map/concatenate | solution.py:59
  168.9 6.2 %copy.21 = f32[512,2800]{1,0:T(8,128)} copy(f32[512,2800]{0,1:T(8,128)} %pad_maximum_fusion) | data formatting | bytes 11468800
  175.2 78.8 %reduce-scatter.10.cloned.1.call-done = f32[32,2800]{1,0:T(8,128)} async-done(((f32[512,2800]{1,0:T(8,128)}), f32[32,2800]{1,0:T(8,128)}) %reduce-scatter.10.cloned.1.call-update) | async-done | bytes 358416
  254.1 1.1 slice.11
  255.1 0.3 copy.27
  255.5 0.9 copy.20
  256.4 0.8 slice.10
  257.2 0.1 copy.26
  257.3 0.7 copy.19
  (17 shorter events, 0.3 us)
Async XLA Ops:
  8.0 56.1 %all-gather.3.cloned.1.call-start = ((), (), s32[]{:S(2)}) async-start(), calls=%async_computation.4 | async-start | bytes 2785280 | tf_op jit(solution)/shard_map/all_gather | solution.py:25
  8.7 90.4 %reduce-scatter.8.cloned.1.call-start = ((), (), s32[]{:S(2)}) async-start(), calls=%async_computation.6 | async-start | bytes 3145728 | tf_op jit(solution)/shard_map/reduce_scatter | solution.py:33
  43.4 1.6 copy-start.1
  43.5 93.3 %all-gather.5.cloned.1.call-start = ((), (), s32[]{:S(2)}) async-start(), calls=%async_computation.7 | async-start | bytes 7372800 | tf_op jit(solution)/shard_map/all_gather | solution.py:15
  46.6 4.8 %copy-start.3 = (f32[1200]{0:T(1024)S(1)}, f32[1200]{0:T(1024)}, u32[]{:S(2)}) copy-start(f32[1200]{0:T(1024)} %param.12) | copy-start | bytes 14404
  46.6 17.5 %copy-start = (bf16[1200,1024]{1,0:T(8,128)(2,1)S(1)}, bf16[1200,1024]{1,0:T(8,128)(2,1)}, u32[]{:S(2)}) copy-start(bf16[1200,1024]{1,0:T(8,128)(2,1)} %param.10) | copy-start | bytes 7372804
  46.6 51.2 %all-to-all-start = ((bf16[64,16,1024]{2,0,1:T(8,128)(2,1)}), bf16[64,16,1024]{2,0,1:T(8,128)(2,1)}, u32[]{:S(2)}, u32[]{:S(2)}) async-start(bf16[64,16,1024]{2,0,1:T(8,128)(2,1)} %bitcast.17), calls=%async_computation.1 | async-start | bytes 4194304 | tf_op jit(solution)/shard_map/all_to_all | solution.py:48
  51.3 108.8 %reduce-scatter.6.cloned.1.call-start = ((), (), s32[]{:S(2)}) async-start(), calls=%async_computation.5 | async-start | bytes 3145728 | tf_op jit(solution)/shard_map/reduce_scatter | solution.py:39
  73.5 2.6 copy-start.2
  76.0 178.0 %reduce-scatter.10.cloned.1.call-start = ((), (), s32[]{:S(2)}) async-start(), calls=%async_computation.8 | async-start | bytes 6127616
Sparse Core Ops, SparseCore 0:
  11.1 52.9 all-gather.2
  65.6 71.0 all-gather.4
  175.3 78.6 reduce-scatter.9
Sparse Core Ops, SparseCore 1:
  43.5 29.3 reduce-scatter.7
  76.1 83.9 reduce-scatter.5
where the time goes:
time: 266 us; the launch traced here: 265 us
  waiting for transfers between devices  146 us (55%)
  blocking collectives  46.9 us (18%)
  local copies, waits for them, and re-layouts  30.6 us (12%)
  matrix products  16.2 us (6%)
  between operations  15.3 us (6%)
  other arithmetic  5.57 us (2%)
  starting transfers between devices  4.92 us (2%)
    unnamed x6, waiting for transfers between devices  80.3 us
    all_gather x1, waiting for transfers between devices, local(): lax.all_gather(orbitals_vir, 'orb', axis=0, tiled=True)  36.1 us
    all_gather x1, blocking collectives, local(): lax.all_gather(slab_occ, 'col', axis=0, tiled=True)  25.2 us
    all_gather x1, blocking collectives, local(): lax.all_gather(orbitals_occ, 'orb', axis=0, tiled=True)  21.7 us
    reduce_scatter x1, waiting for transfers between devices, local(): lax.psum_scatter(part_vir.reshape(shape_three).astype(jnp.bfloat16), 'orb...  16.5 us
    all_gather x1, waiting for transfers between devices, local(): lax.all_gather(slab_vir, 'col', axis=0, tiled=True)  12.7 us
    unnamed x13, local copies, waits for them, and re-layouts  9.13 us
    convert_element_type x2, local copies, waits for them, and re-layouts, local(): part_occ.reshape(shape_three).astype(jnp.bfloat16)  7.07 us
  transfers between devices with their start and end apart: 6, of which 4 were waited for; matrix products, arithmetic and copies ran while one was open for 12% of the time, Pallas kernels for 0%

commit v1 on v0

v1 whole, which is shorter than its diff:
```python
import functools

import jax
import jax.numpy as jnp
from jax import lax
from jax.experimental import pallas as pl
from jax.experimental.pallas import tpu as pltpu
from jax.sharding import PartitionSpec as P

MESH = pl.DeviceIdType.MESH
ANY = pl.BlockSpec(memory_space=pl.ANY)
VMEM = pl.BlockSpec(memory_space=pltpu.VMEM)


def place(n_col):
    me = lax.axis_index("col")
    far, mid, core = me // 4, lax.rem(me // 2, 2), lax.rem(me, 2)
    return me, far, mid, core, lambda f, m, c: (f * 2 + m) * 2 + c


def greet(cols, orbs):
    barrier = pltpu.get_barrier_semaphore()
    for col in cols:
        pl.semaphore_signal(barrier, inc=1, device_id={"col": col}, device_id_type=MESH)
    for orb in orbs:
        pl.semaphore_signal(barrier, inc=1, device_id={"orb": orb}, device_id_type=MESH)
    pl.semaphore_wait(barrier, len(cols) + len(orbs))


def gather_kernel(
    n_col, slab, occ, vir, screen, slabs, peer_occ, peer_vir, screens,
    local_sem, orb_send, orb_recv, slab_send, slab_recv, screen_send, screen_recv,
):
    n_far = n_col // 4
    me, far, mid, core, index = place(n_col)
    part = lax.axis_index("orb")
    other = 1 - part
    others = [lax.rem(me + d, n_col) for d in range(1, n_col)]
    greet(others, [other])

    sends = []

    def push(src, dst, send, recv, device):
        copy = pltpu.make_async_remote_copy(
            src_ref=src, dst_ref=dst, send_sem=send, recv_sem=recv,
            device_id=device, device_id_type=MESH,
        )
        copy.start()
        sends.append(copy)

    push(slab.at[other], slabs.at[1, me], orb_send.at[2], slab_recv.at[1, me], {"orb": other})
    push(vir, peer_vir, orb_send.at[0], orb_recv.at[0], {"orb": other})
    push(occ, peer_occ, orb_send.at[1], orb_recv.at[1], {"orb": other})

    def arrived(k, col):
        ref = slabs.at[k, col]
        pltpu.make_async_remote_copy(
            src_ref=ref, dst_ref=ref, send_sem=orb_send.at[2], recv_sem=slab_recv.at[k, col],
            device_id={"orb": other}, device_id_type=MESH,
        ).wait_recv()

    counter = [0]

    def give(k, col, target, src=None):
        push(
            slabs.at[k, col] if src is None else src, slabs.at[k, col],
            slab_send.at[counter[0]], slab_recv.at[k, col], {"col": target},
        )
        counter[0] += 1

    x_peer, core_peer = index(far, 1 - mid, core), index(far, mid, 1 - core)
    fars = [lax.rem(far + d, n_far) for d in range(1, n_far)]
    own = slab.at[part]
    targets = [index(f, mid, core) for f in fars] + [x_peer, core_peer]
    for target in targets:
        give(0, me, target, own)
    arrived(1, me)
    for target in targets:
        give(1, me, target)
    for n, p in enumerate(others):
        push(screen.at[p], screens.at[me], screen_send.at[n], screen_recv.at[me], {"col": p})
    local = [
        pltpu.make_async_copy(own, slabs.at[0, me], local_sem.at[0]),
        pltpu.make_async_copy(screen.at[me], screens.at[me], local_sem.at[1]),
    ]
    for copy in local:
        copy.start()
    for f in fars:
        col = index(f, mid, core)
        for k in range(2):
            arrived(k, col)
            give(k, col, x_peer)
            give(k, col, core_peer)
    for f in [far] + fars:
        col = index(f, 1 - mid, core)
        for k in range(2):
            arrived(k, col)
            give(k, col, core_peer)
    for f in [far] + fars:
        for m in (mid, 1 - mid):
            for k in range(2):
                arrived(k, index(f, m, 1 - core))
    for p in others:
        ref = screens.at[p]
        pltpu.make_async_remote_copy(
            src_ref=ref, dst_ref=ref, send_sem=orb_send.at[2], recv_sem=screen_recv.at[p],
            device_id={"orb": other}, device_id_type=MESH,
        ).wait_recv()
    for n, ref in ((0, peer_vir), (1, peer_occ)):
        pltpu.make_async_remote_copy(
            src_ref=ref, dst_ref=ref, send_sem=orb_send.at[n], recv_sem=orb_recv.at[n],
            device_id={"orb": other}, device_id_type=MESH,
        ).wait_recv()
    for copy in local:
        copy.wait()
    for copy in sends:
        copy.wait_send()


def gather(n_col, slab, occ, vir, screen):
    n_far = n_col // 4
    dma = pltpu.SemaphoreType.DMA
    n_give = 2 * ((n_far + 1) + 2 * (n_far - 1) + n_far)
    return pl.pallas_call(
        functools.partial(gather_kernel, n_col),
        out_shape=(
            jax.ShapeDtypeStruct((2, n_col) + slab.shape[1:], slab.dtype),
            jax.ShapeDtypeStruct(occ.shape, occ.dtype),
            jax.ShapeDtypeStruct(vir.shape, vir.dtype),
            jax.ShapeDtypeStruct(screen.shape, screen.dtype),
        ),
        in_specs=[ANY] * 4,
        out_specs=(ANY,) * 4,
        scratch_shapes=[
            dma((2,)), dma((3,)), dma((2,)), dma((n_give,)), dma((2, n_col)),
            dma((n_col,)), dma((n_col,)),
        ],
        compiler_params=pltpu.CompilerParams(collective_id=0, has_side_effects=True),
    )(slab, occ, vir, screen)


def scatter_kernel(n_col, pieces, *refs):
    n_far = n_col // 4
    ins, refs = refs[:pieces], refs[pieces:]
    outs, refs = refs[:pieces], refs[pieces:]
    near, out_x, in_x, total, out_far, in_far = [
        refs[i * pieces : (i + 1) * pieces] for i in range(6)
    ]
    near_send, near_recv, x_send, x_recv, far_send, far_recv = refs[6 * pieces :]
    me, far, mid, core, index = place(n_col)
    x_peer, core_peer = index(far, 1 - mid, core), index(far, mid, 1 - core)
    fars = [lax.rem(far + d, n_far) for d in range(1, n_far)]
    greet([core_peer, x_peer] + [index(f, mid, core) for f in fars], [])

    def copy(src, dst, send, recv, target):
        made = pltpu.make_async_remote_copy(
            src_ref=src, dst_ref=dst, send_sem=send, recv_sem=recv,
            device_id={"col": target}, device_id_type=MESH,
        )
        made.start()
        return made

    wide = lambda value: value.astype(jnp.float32)
    first = [[None, None] for t in range(pieces)]
    for t in range(pieces):
        for slot, m in ((0, 1 - mid), (1, mid)):
            first[t][slot] = copy(
                ins[t].at[:, m, 1 - core], near[t].at[slot],
                near_send.at[t, slot], near_recv.at[t, slot], core_peer,
            )
    second = []
    for t in range(pieces):
        first[t][0].wait_recv()
        for f in range(n_far):
            out_x[t][f] = (wide(ins[t][f, 1 - mid, core]) + wide(near[t][0, f])).astype(
                out_x[t].dtype
            )
        second.append(copy(out_x[t], in_x[t], x_send.at[t], x_recv.at[t], x_peer))
        first[t][1].wait_recv()
        for f in range(n_far):
            total[t][f] = wide(ins[t][f, mid, core]) + wide(near[t][1, f])
    third = []
    for t in range(pieces):
        second[t].wait_recv()
        for f in range(n_far):
            total[t][f] = total[t][f] + wide(in_x[t][f])
            out_far[t][f] = total[t][f].astype(out_far[t].dtype)
        for d, f in enumerate(fars):
            third.append(
                copy(
                    out_far[t].at[f], in_far[t].at[d],
                    far_send.at[t, d], far_recv.at[t, d], index(f, mid, core),
                )
            )
    for t in range(pieces):
        value = total[t][far]
        for d in range(n_far - 1):
            third[t * (n_far - 1) + d].wait_recv()
            value = value + wide(in_far[t][d])
        outs[t][...] = value.astype(outs[t].dtype)
    for made in sum(first, []) + second + third:
        made.wait_send()


def scatter(n_col, terms):
    n_far = n_col // 4
    dma = pltpu.SemaphoreType.DMA
    pieces = len(terms)
    block, kind = [t.shape[-2:] for t in terms], terms[0].dtype

    def buffers(lead, dtype=kind):
        return [pltpu.VMEM(lead + b, dtype) for b in block]

    return pl.pallas_call(
        functools.partial(scatter_kernel, n_col, pieces),
        out_shape=[jax.ShapeDtypeStruct(b, kind) for b in block],
        in_specs=[VMEM] * pieces,
        out_specs=[VMEM] * pieces,
        scratch_shapes=buffers((2, n_far))
        + buffers((n_far,))
        + buffers((n_far,))
        + buffers((n_far,), jnp.float32)
        + buffers((n_far,))
        + buffers((n_far - 1,))
        + [
            dma((pieces, 2)), dma((pieces, 2)), dma((pieces,)), dma((pieces,)),
            dma((pieces, n_far - 1)), dma((pieces, n_far - 1)),
        ],
        compiler_params=pltpu.CompilerParams(collective_id=1, has_side_effects=True),
    )(*terms)


def local(slab_occ, slab_vir, orbitals_occ, orbitals_vir, occ_energy, vir_energy, screened):
    n_orb, n_col = lax.axis_size("orb"), lax.axis_size("col")
    part = lax.axis_index("orb")
    block = slab_occ.shape[0] // n_orb
    n_occ, columns = orbitals_occ.shape
    n_vir = orbitals_vir.shape[0]
    kind = slab_occ.dtype
    up = lambda n: -(-n // 128) * 128
    scaled_occ = (slab_occ.astype(jnp.float32) * jnp.exp(occ_energy)[None, :]).astype(kind)
    scaled_vir = (slab_vir.astype(jnp.float32) * jnp.exp(-vir_energy)[None, :]).astype(kind)
    start = up(n_vir)
    slab = jnp.concatenate(
        [
            jnp.pad(scaled_vir, ((0, 0), (0, start - n_vir))),
            jnp.pad(scaled_occ, ((0, 0), (0, up(n_occ) - n_occ))),
        ],
        axis=1,
    ).reshape((n_orb, block, start + up(n_occ)))
    mine = lax.dynamic_slice_in_dim(screened, part * block, block, 0)
    mine = mine.reshape((block, n_col, columns)).transpose((1, 0, 2))
    slabs, peer_occ, peer_vir, screens = gather(n_col, slab, orbitals_occ, orbitals_vir, mine)
    slabs = slabs.reshape((2, n_col * block, slab.shape[2]))
    own_slab, peer_slab = slabs[0], slabs[1]

    def dot(a, b):
        return jnp.dot(a, b, preferred_element_type=jnp.float32)

    green_vir = dot(own_slab[:, :n_vir], orbitals_vir) + dot(peer_slab[:, :n_vir], peer_vir)
    green_occ = dot(own_slab[:, start : start + n_occ], orbitals_occ) + dot(
        peer_slab[:, start : start + n_occ], peer_occ
    )
    screen = screens.reshape((n_col * block, columns)).astype(jnp.float32)
    occ_side = (green_vir * screen).astype(kind)
    vir_side = (green_occ * screen).astype(kind)
    dims = (((1,), (1,)), ((), ()))

    def project(side, orbitals):
        term = lax.dot_general(side, orbitals, dims, preferred_element_type=jnp.float32)
        return term.astype(kind).reshape((n_col // 4, 2, 2, block, orbitals.shape[0]))

    vir_own, vir_peer, occ_own, occ_peer = scatter(
        n_col,
        [
            project(vir_side, orbitals_vir),
            project(vir_side, peer_vir),
            project(occ_side, orbitals_occ),
            project(occ_side, peer_occ),
        ],
    )

    def order(own, peer):
        return jnp.where(
            part == 0, jnp.concatenate([own, peer], 1), jnp.concatenate([peer, own], 1)
        )

    return order(occ_own, occ_peer), order(vir_own, vir_peer)


def solution(mesh):
    return jax.shard_map(
        local,
        mesh=mesh,
        in_specs=(
            P("col", "orb"),
            P("col", "orb"),
            P("orb", "col"),
            P("orb", "col"),
            P("orb"),
            P("orb"),
            P("col", None),
        ),
        out_specs=(P(("col", "orb"), None), P(("col", "orb"), None)),
        check_vma=False,
    )
```

time: 266 us -> 140 us (0.53)
  waiting for transfers between devices: 146 us -> 0 us
  Pallas kernels: 0 us -> 106 us
  blocking collectives: 46.9 us -> 0 us
  local copies, waits for them, and re-layouts: 30.6 us -> 13.2 us
  between operations: 15.3 us -> 0.79 us
  starting transfers between devices: 4.92 us -> 0 us
  matrix products: 16.2 us -> 13.5 us
    pallas_call x0 -> x2, Pallas kernels: none -> 106 us  [the longest x1 73.3 us: gather(): pl.pallas_call(functools.partial(gather_kernel, n_col), out_shape=(jax.Sh...]
    unnamed x6 -> x0, waiting for transfers between devices: 80.3 us -> none
    all_gather x2 -> x0, waiting for transfers between devices: 48.8 us -> none  [the longest x1 36.1 us: local(): lax.all_gather(orbitals_vir, 'orb', axis=0, tiled=True)]
    all_gather x2 -> x0, blocking collectives: 46.9 us -> none  [the longest x1 25.2 us: local(): lax.all_gather(slab_occ, 'col', axis=0, tiled=True)]
    reduce_scatter x2 -> x0, waiting for transfers between devices: 16.5 us -> none  [the longest x1 16.5 us: local(): lax.psum_scatter(part_vir.reshape(shape_three).astype(jnp.bfloat16), 'orb...]
    convert_element_type x4, local copies, waits for them, and re-layouts: 13.1 us -> 6.46 us  [project(): term.astype(kind).reshape((n_col // 4, 2, 2, block, orbitals.shape[0]))]
    unnamed x13 -> x22, local copies, waits for them, and re-layouts: 9.13 us -> 2.55 us
    concatenate x1, other arithmetic: 5.56 us -> 0.72 us  [local(): jnp.concatenate([jnp.pad(scaled_vir, ((0, 0), (0, start - n_vir))), jnp.p...]
  transfers between devices with their start and end apart: 6 -> 0, of which waited for: 4 -> 0; matrix products, arithmetic and copies ran while one was open for 12% -> 0% of each run, Pallas kernels for 0% -> 0%
where the time goes in v1:
time: 140 us
  Pallas kernels  106 us (76%)
  matrix products  13.5 us (10%)
  local copies, waits for them, and re-layouts  13.2 us (9%)
  other arithmetic  6.43 us (5%)
    pallas_call x1, Pallas kernels, gather(): pl.pallas_call(functools.partial(gather_kernel, n_col), out_shape=(jax.Sh...  73.3 us
    pallas_call x1, Pallas kernels, scatter(): pl.pallas_call(functools.partial(scatter_kernel, n_col, pieces), out_shap...  32.6 us
    dot_general x4, matrix products, project(): lax.dot_general(side, orbitals, dims, preferred_element_type=jnp.float32)  7.37 us
    convert_element_type x4, local copies, waits for them, and re-layouts, project(): term.astype(kind).reshape((n_col // 4, 2, 2, block, orbitals.shape[0]))  6.46 us
    dot_general x4, matrix products, dot(): return jnp.dot(a, b, preferred_element_type=jnp.float32)  6.14 us
    select_n x2, other arithmetic, order(): jnp.where(part == 0, jnp.concatenate([own, peer], 1), jnp.concatenate([pe...  3.29 us

profile of v1, /device:TPU:0, one launch (start us, length us, event | category | flops | bytes accessed | tf_op | source)
XLA Modules:
  0.0 139.9 jit_solution(4748607412605427861)
XLA Ops:
  0.6 0.0 copy-start
  0.7 0.8 exp.7
  1.5 0.7 negate_exponential_fusion
  2.2 0.8 multiply_convert_fusion.1
  3.0 0.9 multiply_convert_fusion
  3.9 0.7 fusion.10
  4.6 0.0 copy-done
  4.6 0.1 constant_dynamic-slice_fusion
  4.7 1.1 copy.20
  5.8 73.3 %shard_map.86 = (bf16[2,16,32,1536]{3,2,1,0:T(8,128)(2,1)}, bf16[200,1024]{1,0:T(8,128)(2,1)}, bf16[1200,1024]{1,0:T(8,128)(2,1)}, bf16[16,32,1024]{2,1,0:T(8,128)(2,1)}) custom-call(bf16[2,32,1536]{2,1,0:T(8,128)(2,1)} %bitcast.40, bf16[200,1024]{1,0:T(8,128)(2,1)} %occ.1, bf16[1200,1024]{1,0:T(8,128)(2,1)} %vir.1, bf16[16,32,1024]{2,1,0:T(8,128)(2,1)} %bitcast.31), custom_call_target="tpu_custom_call" | custom-call | tf_op jit(solution)/shard_map/pallas_call | solution.py:124
  79.1 0.0 copy-start.1
  79.1 2.2 %fusion.11 = (bf16[1,16,32,1536]{3,2,1,0:T(8,128)(2,1)S(1)}, bf16[1,16,32,1536]{3,2,1,0:T(8,128)(2,1)S(1)}) fusion(bf16[2,16,32,1536]{3,2,1,0:T(8,128)(2,1)} %get-tuple-element.10), kind=kLoop, calls=%fused_computation.26 | loop fusion | bytes 6291456 | tf_op jit(solution)/shard_map/slice | solution.py:255
  81.4 0.4 copy-done.1
  81.7 1.5 %fusion.3 = f32[512,1024]{1,0:T(8,128)S(1)} fusion(bf16[1200,1024]{1,0:T(8,128)(2,1)S(1)} %copy-done.1, bf16[512,1536]{1,0:T(8,128)(2,1)S(1)} %bitcast.34), kind=kOutput, calls=%fused_computation.7 | convolution fusion | flops 1258291200 | bytes 5865472 | tf_op jit(solution)/shard_map/dot_general | solution.py:258
  83.3 0.0 copy-done.2
  83.3 0.4 copy-done.5
  83.7 0.8 copy-done.9
  84.5 1.6 %fusion.1 = bf16[512,1024]{1,0:T(8,128)(2,1)S(1)} fusion(bf16[512,1024]{1,0:T(8,128)(2,1)S(1)} %bitcast.36, f32[512,1024]{1,0:T(8,128)S(1)} %fusion.3, bf16[1200,1024]{1,0:T(8,128)(2,1)S(1)} %copy-done.9, bf16[512,1536]{1,0:T(8,128)(2,1)S(1)} %bitcast.32), kind=kOutput, calls=%fused_computation.5 | convolution fusion | flops 1260388352 | bytes 7962624 | tf_op jit(solution)/shard_map/dot_general | solution.py:258
  86.1 1.2 convolution_convert_fusion.2
  87.3 1.2 convolution_convert_fusion.3
  88.5 1.8 %copy.16 = bf16[512,200]{1,0:T(8,128)(2,1)} copy(bf16[512,200]{0,1:T(8,128)(2,1)} %convolution_convert_fusion.3) | data formatting | bytes 409600 | tf_op jit(solution)/shard_map/convert_element_type | solution.py:271
  90.3 1.8 %copy.17 = bf16[512,200]{1,0:T(8,128)(2,1)} copy(bf16[512,200]{0,1:T(8,128)(2,1)} %convolution_convert_fusion.2) | data formatting | bytes 409600 | tf_op jit(solution)/shard_map/convert_element_type | solution.py:271
  92.1 1.4 %fusion.8 = f32[512,1024]{1,0:T(8,128)S(1)} fusion(bf16[200,1024]{1,0:T(8,128)(2,1)S(1)} %copy-done.4, bf16[512,1536]{1,0:T(8,128)(2,1)} %bitcast.35), kind=kOutput, calls=%fused_computation.18 | convolution fusion | flops 209715200 | bytes 2768896 | tf_op jit(solution)/shard_map/dot_general | solution.py:258
  93.5 1.6 %fusion = bf16[512,1024]{1,0:T(8,128)(2,1)S(1)} fusion(bf16[512,1024]{1,0:T(8,128)(2,1)S(1)} %bitcast.37, f32[512,1024]{1,0:T(8,128)S(1)} %fusion.8, bf16[200,1024]{1,0:T(8,128)(2,1)S(1)} %copy-done.8, bf16[512,1536]{1,0:T(8,128)(2,1)} %bitcast.33), kind=kOutput, calls=%fused_computation.4 | convolution fusion | flops 211812352 | bytes 4866048 | tf_op jit(solution)/shard_map/dot_general | solution.py:258
  95.1 0.9 copy-done.6
  96.1 1.5 %convolution_convert_fusion = bf16[512,1200]{0,1:T(8,128)(2,1)S(1)} fusion(bf16[512,1024]{1,0:T(8,128)(2,1)S(1)} %fusion, bf16[1200,1024]{1,0:T(8,128)(2,1)S(1)} %copy-done.10), kind=kOutput, calls=%fused_computation | convolution fusion | flops 1258905600 | bytes 4734976 | tf_op jit(solution)/shard_map/dot_general | solution.py:270
  97.5 1.5 %copy.15 = bf16[512,1200]{1,0:T(8,128)(2,1)} copy(bf16[512,1200]{0,1:T(8,128)(2,1)S(1)} %convolution_convert_fusion) | data formatting | bytes 2457600 | tf_op jit(solution)/shard_map/convert_element_type | solution.py:271
  99.0 3.5 %convolution_convert_fusion.1 = bf16[512,1200]{0,1:T(8,128)(2,1)S(1)} fusion(bf16[512,1024]{1,0:T(8,128)(2,1)} %copy-done.6, bf16[1200,1024]{1,0:T(8,128)(2,1)} %vir.1), kind=kOutput, calls=%fused_computation.1 | convolution fusion | flops 1258905600 | bytes 4734976 | tf_op jit(solution)/shard_map/dot_general | solution.py:270
  102.5 1.5 %copy.14 = bf16[512,1200]{1,0:T(8,128)(2,1)} copy(bf16[512,1200]{0,1:T(8,128)(2,1)S(1)} %convolution_convert_fusion.1) | data formatting | bytes 2457600 | tf_op jit(solution)/shard_map/convert_element_type | solution.py:271
  104.0 32.6 %shard_map.87 = (bf16[32,1200]{1,0:T(8,128)(2,1)}, bf16[32,1200]{1,0:T(8,128)(2,1)}, bf16[32,200]{1,0:T(8,128)(2,1)}, bf16[32,200]{1,0:T(8,128)(2,1)}) custom-call(bf16[4,2,2,32,1200]{4,3,2,1,0:T(8,128)(2,1)} %bitcast.29, bf16[4,2,2,32,1200]{4,3,2,1,0:T(8,128)(2,1)} %bitcast.28, bf16[4,2,2,32,200]{4,3,2,1,0:T(8,128)(2,1)} %bitcast.38, ...), custom_call_target="tpu_custom_call" | custom-call | tf_op jit(solution)/shard_map/pallas_call | solution.py:214
  136.6 1.5 %maximum_select_fusion.1 = bf16[32,400]{1,0:T(8,128)(2,1)} fusion(bf16[32,200]{1,0:T(8,128)(2,1)} %get-tuple-element.15, bf16[32,200]{1,0:T(8,128)(2,1)} %get-tuple-element.14, pred[]{:T(512)S(6)} %eq.4), kind=kLoop, calls=%fused_computation.23 | loop fusion | flops 115200 | bytes 51201 | tf_op jit(solution)/shard_map/jit(_where)/select_n | solution.py:284
  138.1 1.8 %maximum_select_fusion = bf16[32,2400]{1,0:T(8,128)(2,1)} fusion(bf16[32,1200]{1,0:T(8,128)(2,1)} %get-tuple-element.17, bf16[32,1200]{1,0:T(8,128)(2,1)} %get-tuple-element.16, pred[]{:T(512)S(6)} %eq.4), kind=kLoop, calls=%fused_computation.21 | loop fusion | flops 691200 | bytes 307201 | tf_op jit(solution)/shard_map/jit(_where)/select_n | solution.py:284
  (14 shorter events, 0.0 us)
Async XLA Ops:
  0.6 4.0 %copy-start = (bf16[64,16384]{1,0:T(8,128)(2,1)S(1)}, bf16[64,16384]{1,0:T(8,128)(2,1)}, u32[]{:S(2)}) copy-start(bf16[64,16384]{1,0:T(8,128)(2,1)} %param.13) | copy-start | bytes 6291460
  79.1 2.6 %copy-start.1 = (bf16[1200,1024]{1,0:T(8,128)(2,1)S(1)}, bf16[1200,1024]{1,0:T(8,128)(2,1)}, u32[]{:S(2)}) copy-start(bf16[1200,1024]{1,0:T(8,128)(2,1)} %vir.1) | copy-start | bytes 7372804
  81.4 1.9 %copy-start.2 = (bf16[1,16,32,1536]{3,2,1,0:T(8,128)(2,1)}, bf16[1,16,32,1536]{3,2,1,0:T(8,128)(2,1)S(1)}, u32[]{:S(2)}) copy-start(bf16[1,16,32,1536]{3,2,1,0:T(8,128)(2,1)S(1)} %get-tuple-element.18) | copy-start | bytes 4718596
  81.4 1.9 %copy-start.3 = (bf16[1,16,32,1536]{3,2,1,0:T(8,128)(2,1)}, bf16[1,16,32,1536]{3,2,1,0:T(8,128)(2,1)S(1)}, u32[]{:S(2)}) copy-start(bf16[1,16,32,1536]{3,2,1,0:T(8,128)(2,1)S(1)} %get-tuple-element.19) | copy-start | bytes 4718596
  81.7 2.0 %copy-start.5 = (bf16[16,32,1024]{2,1,0:T(8,128)(2,1)S(1)}, bf16[16,32,1024]{2,1,0:T(8,128)(2,1)}, u32[]{:S(2)}) copy-start(bf16[16,32,1024]{2,1,0:T(8,128)(2,1)} %get-tuple-element.12) | copy-start | bytes 3145732
  81.7 2.7 %copy-start.9 = (bf16[1200,1024]{1,0:T(8,128)(2,1)S(1)}, bf16[1200,1024]{1,0:T(8,128)(2,1)}, u32[]{:S(2)}) copy-start(bf16[1200,1024]{1,0:T(8,128)(2,1)} %get-tuple-element.13) | copy-start | bytes 7372804
  84.5 1.6 %copy-start.7 = (bf16[200,1024]{1,0:T(8,128)(2,1)S(1)}, bf16[200,1024]{1,0:T(8,128)(2,1)}, u32[]{:S(2)}) copy-start(bf16[200,1024]{1,0:T(8,128)(2,1)} %get-tuple-element.11) | copy-start | bytes 1228804
  84.5 2.9 %copy-start.4 = (bf16[200,1024]{1,0:T(8,128)(2,1)S(1)}, bf16[200,1024]{1,0:T(8,128)(2,1)}, u32[]{:S(2)}) copy-start(bf16[200,1024]{1,0:T(8,128)(2,1)} %occ.1) | copy-start | bytes 1228804
  92.1 1.4 %copy-start.8 = (bf16[200,1024]{1,0:T(8,128)(2,1)S(1)}, bf16[200,1024]{1,0:T(8,128)(2,1)}, u32[]{:S(2)}) copy-start(bf16[200,1024]{1,0:T(8,128)(2,1)} %get-tuple-element.11) | copy-start | bytes 1228804
  93.5 2.5 %copy-start.10 = (bf16[1200,1024]{1,0:T(8,128)(2,1)S(1)}, bf16[1200,1024]{1,0:T(8,128)(2,1)}, u32[]{:S(2)}) copy-start(bf16[1200,1024]{1,0:T(8,128)(2,1)} %get-tuple-element.13) | copy-start | bytes 7372804
  95.1 1.0 copy-start.6
